TPU v7x, 256 devices: a whole 4x4x8 slice. The times are simulated.
256 devices in a mesh: dp: 16 (over z_hi, x), rows: 16 (over y, z_lo, core).
Axes of the slice: x: 4, y: 4, z: 8 (z_hi: 4, z_lo: 2; z = z_hi * 2 + z_lo), core: 2. Of those that a mesh axis runs over, the one named last changes fastest.
Arguments:
- features: bfloat16 [16, 128, 32, 1536], P('dp', 'rows'), may hold values from -6 to 6
- kernel: bfloat16 [7, 7, 1536], replicated, may hold values from -0.875 to 0.875
- ln_gain: float32 [1536], replicated, may hold values from 0.1 to 1.9
- layer_scale: float32 [1536], replicated, may hold values from 0.2 to 1
- w_in: bfloat16 [1536, 3072], P(('dp', 'rows')), may hold values from -0.15625 to 0.15625
- w_out: bfloat16 [3072, 1536], P(('dp', 'rows')), may hold values from -0.109375 to 0.109375
- pairs: int32 [16], replicated, may hold values from 0 to 15, as said below
- negatives: int32 [16, 32, 8, 8], P('dp', 'rows'), may hold values from 0 to 127
Outputs:
- grad_features: bfloat16 [16, 128, 32, 1536], P('dp', 'rows')
- grad_kernel: float32 [7, 7, 1536], replicated
- loss: float32 [], replicated
Inputs may be any that keep to these rules, and one draw needn't show every extreme that they name: pairs[pairs[i]] == i and pairs[i] != i: the images form 16 / 2 preference pairs.
All inputs are finite; a program needn't handle non-finite values.
Results may differ from a plain program's by a relative error of at most 0.014.
Values may be sent and summed in bfloat16 or wider, within the bound.
No kernel may reach another device: no remote copies, remote signals or barrier semaphores. Data moves between devices by JAX's collectives and lax.ppermute only.
A program may use at most 128 MiB of HBM per device.

v0:
```python
import jax
import jax.numpy as jnp
from jax import lax
from jax.sharding import PartitionSpec as P

REGION = 4
NEG = 8
loss_scale = 1024.0
inv_temp = 16.0
eps_layer = 1e-06
eps_norm = 1e-06


def padded_2(cells, sides, width):
    for axis, dim in sides:
        count = lax.axis_size(axis)
        ends = count - 1
        head = lax.slice_in_dim(cells, 0, width, axis=dim)
        tail = lax.slice_in_dim(cells, cells.shape[dim] - width, cells.shape[dim], axis=dim)
        cells = jnp.concatenate(
            [
                lax.ppermute(tail, axis, [(i, (i + 1) % count) for i in range(ends)]),
                cells,
                lax.ppermute(head, axis, [((i + 1) % count, i) for i in range(ends)]),
            ],
            axis=dim,
        )
    return cells


def depthwise(padded, kernel, height, breadth):
    summed = jnp.zeros((padded.shape[0], height, breadth, padded.shape[3]), jnp.float32)
    for offset_row in range(7):
        for offset_col in range(7):
            window = padded[
                :, offset_row : offset_row + height, offset_col : offset_col + breadth, :
            ]
            summed = summed + window.astype(jnp.float32) * kernel[offset_row, offset_col].astype(
                jnp.float32
            )
    return summed


def kernel_terms(padded, grad_conv, height, breadth):
    grad_float = grad_conv.astype(jnp.float32)
    stacked = []
    for offset_row in range(7):
        row_terms = []
        for offset_col in range(7):
            window = padded[
                :, offset_row : offset_row + height, offset_col : offset_col + breadth, :
            ]
            row_terms.append(jnp.sum(window.astype(jnp.float32) * grad_float, axis=(0, 1, 2)))
        stacked.append(jnp.stack(row_terms))
    return jnp.stack(stacked)


def gelu_parts(pre_act):
    normal_cdf = 0.5 * (1.0 + jax.scipy.special.erf(pre_act * 0.7071067811865476))
    density = jnp.exp(-0.5 * pre_act * pre_act) * 0.3989422804014327
    return (pre_act * normal_cdf, normal_cdf + pre_act * density)


def norm_rows(conv_rows):
    centred = conv_rows - jnp.mean(conv_rows, axis=-1, keepdims=True)
    spread = jnp.sqrt(jnp.mean(centred * centred, axis=-1, keepdims=True) + eps_layer)
    return (centred / spread, spread)


def body(features, kernel, ln_gain, layer_scale, w_in, w_out, pairs, negatives):
    height, breadth, channels = (features.shape[1], features.shape[2], features.shape[3])
    w_in_all, w_out_all = (
        lax.all_gather(w_in, ("dp", "rows"), axis=0, tiled=True),
        lax.all_gather(w_out, ("dp", "rows"), axis=0, tiled=True),
    )
    rimmed = padded_2(features, (("rows", 1),), 3)
    padded = jnp.pad(rimmed, ((0, 0), (0, 0), (3, 3), (0, 0)))
    conv_rows = depthwise(padded, kernel, height, breadth).reshape(-1, channels)
    unit_rows, spread = norm_rows(conv_rows)
    normed = (unit_rows * ln_gain).astype(jnp.bfloat16)
    pre_act = jnp.dot(normed, w_in_all, preferred_element_type=jnp.float32)
    activated, gelu_slope = gelu_parts(pre_act)
    hidden = activated.astype(jnp.bfloat16)
    mixed_rows = jnp.dot(hidden, w_out_all, preferred_element_type=jnp.float32)
    block_out = features.reshape(-1, channels).astype(jnp.float32) + layer_scale * mixed_rows
    reg_rows, reg_cols = (height // REGION, breadth // REGION)
    pooled = jnp.mean(block_out.reshape(reg_rows, REGION, reg_cols, REGION, channels), axis=(1, 3))
    inv_norm = lax.rsqrt(jnp.sum(pooled * pooled, axis=-1, keepdims=True) + eps_norm)
    unit_tok = pooled * inv_norm
    tokens_b = unit_tok.astype(jnp.bfloat16)
    gathered = lax.all_gather(tokens_b[None], "dp", axis=0, tiled=True)
    images = gathered.shape[0]
    keys_flat = gathered.transpose(1, 0, 2, 3).reshape(reg_rows, images * reg_cols, channels)
    my_image = lax.axis_index("dp")
    partner = lax.dynamic_index_in_dim(pairs, my_image, keepdims=False)
    columns = jnp.arange(reg_cols, dtype=jnp.int32)
    positive = jnp.broadcast_to(
        (partner * reg_cols + columns)[None, :, None], (reg_rows, reg_cols, 1)
    )
    chosen = jnp.concatenate([positive, negatives[0]], axis=2)
    one_hot = (chosen[..., None] == jnp.arange(images * reg_cols, dtype=jnp.int32)).astype(
        jnp.float32
    )
    similar = jnp.einsum("rtc,rjc->rtj", tokens_b, keys_flat, preferred_element_type=jnp.float32)
    logits = inv_temp * jnp.sum(one_hot * similar[:, :, None, :], axis=-1)
    exp_logits = jnp.exp(logits)
    denominator = jnp.sum(exp_logits, axis=-1, keepdims=True)
    loss_tok = jnp.log(denominator[..., 0]) - logits[..., 0]
    first_slot = (jnp.arange(NEG + 1) == 0).astype(jnp.float32)
    slot_coef = loss_scale * inv_temp * (exp_logits / denominator - first_slot)
    weight_map = jnp.sum(slot_coef[..., None] * one_hot, axis=2)
    anchor = jnp.einsum(
        "rtj,rjc->rtc", weight_map, keys_flat.astype(jnp.float32), precision=lax.Precision.HIGHEST
    )
    weight_four = weight_map.reshape(reg_rows, reg_cols, images, reg_cols)
    key_table = jnp.einsum(
        "rtiu,rtc->iruc", weight_four, tokens_b.astype(jnp.float32), precision=lax.Precision.HIGHEST
    )
    own_grads = lax.psum_scatter(
        key_table.astype(jnp.bfloat16), "dp", scatter_dimension=0, tiled=True
    ).astype(jnp.float32)[0]
    grad_tok = anchor + own_grads
    grad_pool = (
        grad_tok - unit_tok * jnp.sum(unit_tok * grad_tok, axis=-1, keepdims=True)
    ) * inv_norm
    scaled = grad_pool / float(REGION * REGION)
    grad_out = jnp.broadcast_to(
        scaled[:, None, :, None, :], (reg_rows, REGION, reg_cols, REGION, channels)
    ).reshape(height * breadth, channels)
    grad_mix = (layer_scale * grad_out).astype(jnp.bfloat16)
    grad_hid = lax.dot_general(
        grad_mix, w_out_all, (((1,), (1,)), ((), ())), preferred_element_type=jnp.float32
    )
    grad_pre = (grad_hid * gelu_slope).astype(jnp.bfloat16)
    grad_norm = lax.dot_general(
        grad_pre, w_in_all, (((1,), (1,)), ((), ())), preferred_element_type=jnp.float32
    )
    grad_unit = grad_norm * ln_gain
    mean_one = jnp.mean(grad_unit, axis=-1, keepdims=True)
    mean_two = jnp.mean(grad_unit * unit_rows, axis=-1, keepdims=True)
    grad_conv = (
        ((grad_unit - mean_one - unit_rows * mean_two) / spread)
        .astype(jnp.bfloat16)
        .reshape(1, height, breadth, channels)
    )
    flipped = kernel[::-1, ::-1]
    grad_rim = padded_2(grad_conv, (("rows", 1),), 3)
    grad_pad = jnp.pad(grad_rim, ((0, 0), (0, 0), (3, 3), (0, 0)))
    conv_back = depthwise(grad_pad, flipped, height, breadth)
    grad_features = (grad_out.reshape(1, height, breadth, channels) + conv_back).astype(
        jnp.bfloat16
    )
    kernel_local = kernel_terms(padded, grad_conv, height, breadth)
    grad_kernel, loss_sum = lax.psum((kernel_local, jnp.sum(loss_tok)), ("dp", "rows"))
    token_count = lax.axis_size("dp") * lax.axis_size("rows") * reg_rows * reg_cols
    loss = loss_sum / float(token_count)
    return (grad_features, grad_kernel, loss)


def solution(mesh):
    return jax.shard_map(
        body,
        mesh=mesh,
        in_specs=(
            P("dp", "rows", None, None),
            P(),
            P(),
            P(),
            P(("dp", "rows"), None),
            P(("dp", "rows"), None),
            P(),
            P("dp", "rows", None, None),
        ),
        out_specs=(P("dp", "rows", None, None), P(), P()),
        check_vma=False,
    )
```

profile of v0, /device:TPU:1, one launch (start us, length us, event | category | flops | bytes accessed | tf_op | source)
XLA Modules:
  0.0 1320.9 jit_solution(3228387225316494650)
XLA Ops:
  9.8 4.9 collective-permute-start
  14.7 1.9 collective-permute-start.1
  16.7 1.2 dynamic_slice.4
  24.4 13.8 %fusion.158 = (f32[8,32]{1,0:T(8,128)S(1)}, f32[1,8,32,1536]{3,2,1,0:T(8,128)}) fusion(f32[1536]{0:T(1024)S(1)} %get-tuple-element.110, bf16[1,14,38,1536]{3,2,1,0:T(8,128)(2,1)S(1)} %select_maximum_fusion.2, f32[1536]{0:T(1024)S(1)} %get-tuple-element.111, f32[1536]{0:T(1024)S(1)} %get-tuple-element.64, f32[1536]{0:T(1024)S(1)} %get-tuple-element.65, ...), kind=kLoop, calls=%fused_computation.367 | loop fusion | flops 57802496 | bytes 40410112 | tf_op jit(solution)/shard_map/reduce_sum | solution.py:65
  38.3 1.7 multiply_reduce_fusion.1
  40.1 2.8 fusion.136
  42.9 392.4 %all-gather.5.cloned.1.call-done = bf16[256,6,3072]{2,1,0:T(8,128)(2,1)} async-done(((bf16[1,6,3072]{2,1,0:T(8,128)(2,1)}), bf16[256,6,3072]{2,1,0:T(8,128)(2,1)}) %all-gather.5.cloned.1.call-update) | async-done | bytes 9437200 | tf_op jit(solution)/shard_map/all_gather | solution.py:73
  435.3 14.2 %reshape.776 = bf16[1536,3072]{1,0:T(8,128)(2,1)} reshape(bf16[256,6,3072]{2,1,0:T(8,128)(2,1)} %all-gather.5.cloned.1.call-done) | data formatting | bytes 18874368
  449.5 8.5 fusion.141
  458.0 399.4 %all-gather.7.cloned.1.call-done = bf16[256,12,1536]{2,1,0:T(8,128)(2,1)} async-done(((bf16[1,12,1536]{2,1,0:T(8,128)(2,1)}), bf16[256,12,1536]{2,1,0:T(8,128)(2,1)}) %all-gather.7.cloned.1.call-update) | async-done | bytes 9437200 | tf_op jit(solution)/shard_map/all_gather | solution.py:74
  857.4 15.0 %reshape.778 = bf16[3072,1536]{1,0:T(8,128)(2,1)} reshape(bf16[256,12,1536]{2,1,0:T(8,128)(2,1)} %all-gather.7.cloned.1.call-done) | data formatting | bytes 18874368
  872.4 8.5 fusion.7
  880.9 2.7 reshape.719
  883.6 1.8 reduce_sum.544
  885.6 36.9 %all_gather.11 = bf16[16,2,8,1536]{3,2,1,0:T(8,128)(2,1)S(1)} all-gather(bf16[1,2,8,1536]{3,2,1,0:T(8,128)(2,1)S(1)} %fusion.150), channel_id=1, replica_groups=mesh['dp'=16,'rows'=16] {'dp'}, dimensions={0}, use_global_device_ids=true | all-gather | bytes 835584 | tf_op jit(solution)/shard_map/all_gather | solution.py:91
  924.3 1.7 fusion.8
  926.8 84.5 %psum.15 = f32[]{:T(128)} all-reduce(f32[]{:T(128)} %subtract_reduce_fusion), channel_id=1, replica_groups=mesh['dp'=16,'rows'=16] {'dp','rows'}, use_global_device_ids=true, to_apply=%region_62.63 | all-reduce | flops 1 | bytes 8 | tf_op jit(solution)/shard_map/psum | solution.py:154
  1012.0 6.6 reduce-scatter.2.cloned.1.call-done
  1018.6 1.6 convolution_add_fusion
  1020.5 1.4 broadcast_in_dim.5
  1021.9 2.8 reshape.722
  1024.7 2.8 reshape_reshape.3
  1027.4 12.4 fusion.157
  1039.9 6.2 fusion.135
  1046.1 2.5 fusion.132
  1048.6 4.0 fusion.114
  1054.5 4.8 collective-permute-start.2
  1059.4 2.1 collective-permute-start.3
  1063.1 5.5 collective-permute-done.3
  1069.5 12.2 add_convert_fusion
  1081.6 229.9 %all-reduce.4.cloned.1.call-done = f32[7,7,1536]{2,1,0:T(8,128)} async-done(((f32[7,7,1536]{2,1,0:T(8,128)}), f32[7,7,1536]{2,1,0:T(8,128)}) %all-reduce.4.cloned.1.call-update) | async-done | bytes 301072 | tf_op jit(solution)/shard_map/psum | solution.py:154
  1311.5 1.7 copy.48
  (258 shorter events, 14.5 us)
Async XLA Ops:
  7.2 15.0 %copy-start.4 = (bf16[1,8,32,1536]{3,2,1,0:T(8,128)(2,1)S(1)}, bf16[1,8,32,1536]{3,2,1,0:T(8,128)(2,1)}, u32[]{:S(2)}) copy-start(bf16[1,8,32,1536]{3,2,1,0:T(8,128)(2,1)} %param.8) | copy-start | bytes 2359300
  7.2 14.0 %copy-start.9 = (bf16[7,7,1536]{2,1,0:T(8,128)(2,1)S(1)}, bf16[7,7,1536]{2,1,0:T(8,128)(2,1)}, u32[]{:S(2)}) copy-start(bf16[7,7,1536]{2,1,0:T(8,128)(2,1)} %param.9) | copy-start | bytes 451588
  7.2 428.1 %all-gather.5.cloned.1.call-start = ((), (), s32[]{:S(2)}) async-start(), calls=%async_computation.3 | async-start | bytes 12632064 | tf_op jit(solution)/shard_map/all_gather | solution.py:73
  7.9 849.5 %all-gather.7.cloned.1.call-start = ((), (), s32[]{:S(2)}) async-start(), calls=%async_computation.4 | async-start | bytes 12632064 | tf_op jit(solution)/shard_map/all_gather | solution.py:74
  8.7 1009.9 %reduce-scatter.2.cloned.1.call-start = ((), (), s32[]{:S(2)}) async-start(), calls=%async_computation.1 | async-start | bytes 835584 | tf_op jit(solution)/shard_map/reduce_scatter | solution.py:119
  9.8 12.4 collective-permute-start
  14.7 8.1 collective-permute-start.1
  42.9 406.6 %copy-start.74 = (f32[1536]{0:T(1024)S(1)}, f32[1536]{0:T(1024)}, u32[]{:S(2)}) copy-start(f32[1536]{0:T(1024)} %param.10) | copy-start | bytes 18436
  458.0 414.4 %copy-start.75 = (f32[1536]{0:T(1024)S(1)}, f32[1536]{0:T(1024)}, u32[]{:S(2)}) copy-start(f32[1536]{0:T(1024)} %param.11) | copy-start | bytes 18436
  883.6 40.3 %copy-start.73 = (f32[9]{0:T(128)S(1)}, f32[9]{0:T(128)}, u32[]{:S(2)}) copy-start(f32[9]{0:T(128)} %compare_convert_fusion) | copy-start | bytes 112
  926.0 385.5 %all-reduce.4.cloned.1.call-start = ((), (), s32[]{:S(2)}) async-start(), calls=%async_computation.2 | async-start | bytes 688128 | tf_op jit(solution)/shard_map/psum | solution.py:154
  1053.1 15.6 %copy-start.1 = (bf16[256,1536]{1,0:T(8,128)(2,1)S(1)}, bf16[256,1536]{1,0:T(8,128)(2,1)}, u32[]{:S(2)}) copy-start(bf16[256,1536]{1,0:T(8,128)(2,1)} %copy-done) | copy-start | bytes 2359300
  1054.5 8.6 collective-permute-start.2
  1059.4 9.3 collective-permute-start.3
  1062.8 6.3 copy-start.8
  1062.8 6.3 copy-start.12
  1062.8 6.3 copy-start.14
  1062.8 6.3 copy-start.16
  1062.9 6.3 copy-start.18
  1062.9 6.3 copy-start.20
  1062.9 6.3 copy-start.22
  1062.9 6.3 copy-start.24
  1062.9 6.3 copy-start.26
  1062.9 6.3 copy-start.28
  1062.9 6.3 copy-start.30
  1062.9 6.3 copy-start.32
  1062.9 6.3 copy-start.34
  1062.9 6.3 copy-start.36
  1063.0 6.3 copy-start.38
  1063.0 6.3 copy-start.40
  1063.0 6.3 copy-start.42
  1063.0 6.3 copy-start.44
  (52 other events, 183.0 us)
Sparse Core Ops, SparseCore 0:
  9.9 425.3 all-gather.4
  437.2 420.2 all-gather.6
  926.1 92.4 reduce-scatter.1
  1062.9 248.5 all-reduce.3
where the time goes:
time: 1320 us
  waiting for transfers between devices  1040 us (79%)
  blocking collectives  121 us (9%)
  other arithmetic  50.6 us (4%)
  local copies, waits for them, and re-layouts  48.1 us (4%)
  matrix products  33 us (2%)
  between operations  17.9 us (1%)
  starting transfers between devices  14.2 us (1%)
    all_gather x1, waiting for transfers between devices, body(): lax.all_gather(w_out, ('dp', 'rows'), axis=0, tiled=True)  399 us
    all_gather x1, waiting for transfers between devices, body(): lax.all_gather(w_in, ('dp', 'rows'), axis=0, tiled=True)  392 us
    psum x1, waiting for transfers between devices, body(): lax.psum((kernel_local, jnp.sum(loss_tok)), ('dp', 'rows'))  230 us
    psum x1, blocking collectives, body(): lax.psum((kernel_local, jnp.sum(loss_tok)), ('dp', 'rows'))  84.5 us
    all_gather x1, blocking collectives, body(): gathered = lax.all_gather(tokens_b[None], 'dp', axis=0, tiled=True)  36.9 us
    unnamed x162, local copies, waits for them, and re-layouts  33.6 us
  transfers between devices with their start and end apart: 8, of which 6 were waited for; matrix products, arithmetic and copies ran while one was open for 5% of the time, Pallas kernels for 0%

commit v1 on v0

--- a/solution.py
+++ b/solution.py
@@ -71,7 +71,12 @@
     height, breadth, channels = (features.shape[1], features.shape[2], features.shape[3])
     w_in_all, w_out_all = (
         lax.all_gather(w_in, ("dp", "rows"), axis=0, tiled=True),
-        lax.all_gather(w_out, ("dp", "rows"), axis=0, tiled=True),
+        jnp.concatenate(
+            lax.all_to_all(
+                jnp.stack([w_out] * lax.axis_size(("dp", "rows"))), ("dp", "rows"), 0, 0
+            ),
+            axis=0,
+        ),
     )
     rimmed = padded_2(features, (("rows", 1),), 3)
     padded = jnp.pad(rimmed, ((0, 0), (0, 0), (3, 3), (0, 0)))

time: 1320 us -> 1070 us (0.81)
  waiting for transfers between devices: 1040 us -> 695 us
  local copies, waits for them, and re-layouts: 48.1 us -> 99.9 us
  starting transfers between devices: 14.2 us -> 29.9 us
  blocking collectives: 121 us -> 135 us
    all_gather x1 -> x0, waiting for transfers between devices: 399 us -> none  [body(): lax.all_gather(w_out, ('dp', 'rows'), axis=0, tiled=True)]
    ppermute x2, waiting for transfers between devices: 0.01 us -> 303 us  [padded_2(): lax.ppermute(tail, axis, [(i, (i + 1) % count) for i in range(ends)])]
    all_gather x1, waiting for transfers between devices: 392 us -> 146 us  [body(): lax.all_gather(w_in, ('dp', 'rows'), axis=0, tiled=True)]
    another operation x56, local copies, waits for them, and re-layouts: 0.85 us -> 49.8 us  [kernel_terms(): stacked.append(jnp.stack(row_terms))]
    all_to_all x0 -> x1, starting transfers between devices: none -> 16.5 us  [body(): lax.all_to_all(jnp.stack([w_out] * lax.axis_size(('dp', 'rows'))), ('dp',...]
    unnamed x162 -> x163, local copies, waits for them, and re-layouts: 33.6 us -> 17.9 us
  transfers between devices with their start and end apart: 8 -> 8, of which waited for: 6 -> 5; matrix products, arithmetic and copies ran while one was open for 5% -> 11% of each run, Pallas kernels for 0% -> 0%
where the time goes in v1:
time: 1070 us; the launch traced here: 1060 us
  waiting for transfers between devices  695 us (65%)
  blocking collectives  135 us (13%)
  local copies, waits for them, and re-layouts  99.9 us (9%)
  other arithmetic  51.8 us (5%)
  matrix products  32.9 us (3%)
  starting transfers between devices  29.9 us (3%)
  between operations  17.6 us (2%)
    ppermute x2, waiting for transfers between devices, padded_2(): lax.ppermute(tail, axis, [(i, (i + 1) % count) for i in range(ends)])  303 us
    psum x1, waiting for transfers between devices, body(): lax.psum((kernel_local, jnp.sum(loss_tok)), ('dp', 'rows'))  234 us
    all_gather x1, waiting for transfers between devices, body(): lax.all_gather(w_in, ('dp', 'rows'), axis=0, tiled=True)  146 us
    psum x1, blocking collectives, body(): lax.psum((kernel_local, jnp.sum(loss_tok)), ('dp', 'rows'))  87.4 us
    another operation x56, local copies, waits for them, and re-layouts, kernel_terms(): stacked.append(jnp.stack(row_terms))  49.8 us
    all_gather x1, blocking collectives, body(): gathered = lax.all_gather(tokens_b[None], 'dp', axis=0, tiled=True)  47.5 us
  transfers between devices with their start and end apart: 8, of which 5 were waited for; matrix products, arithmetic and copies ran while one was open for 11% of the time, Pallas kernels for 0%

profile of v1, /device:TPU:1, one launch (start us, length us, event | category | flops | bytes accessed | tf_op | source)
XLA Modules:
  0.0 1062.1 jit_solution(9285686645904140276)
XLA Ops:
  7.9 6.9 stack.130
  14.8 16.5 %all-to-all-start = ((bf16[256,12,1536]{2,1,0:T(8,128)(2,1)}), bf16[256,12,1536]{2,1,0:T(8,128)(2,1)}, u32[]{:S(2)}, u32[]{:S(2)}) async-start(bf16[256,12,1536]{2,1,0:T(8,128)(2,1)} %stack.130), calls=%async_computation | async-start | bytes 25165824 | tf_op jit(solution)/shard_map/all_to_all | solution.py:75
  31.4 4.1 collective-permute-start.1
  35.5 2.1 collective-permute-start
  40.8 302.6 %collective-permute-done = bf16[1,3,32,1536]{3,2,1,0:T(8,128)(2,1)S(1)} collective-permute-done((bf16[1,3,32,1536]{3,2,1,0:T(8,128)(2,1)S(1)}, bf16[1,3,32,1536]{3,2,1,0:T(8,128)(2,1)S(1)}, u32[]{:S(2)}, u32[]{:S(2)}) %collective-permute-start) | collective-permute-done | bytes 294944 | tf_op jit(solution)/shard_map/ppermute | solution.py:22
  343.5 6.0 collective-permute-done.1
  350.4 13.8 %fusion.157 = (f32[8,32]{1,0:T(8,128)S(1)}, f32[1,8,32,1536]{3,2,1,0:T(8,128)}) fusion(f32[1536]{0:T(1024)S(1)} %get-tuple-element.110, bf16[1,14,38,1536]{3,2,1,0:T(8,128)(2,1)S(1)} %select_maximum_fusion.2, f32[1536]{0:T(1024)S(1)} %get-tuple-element.111, f32[1536]{0:T(1024)S(1)} %get-tuple-element.64, f32[1536]{0:T(1024)S(1)} %get-tuple-element.65, ...), kind=kLoop, calls=%fused_computation.366 | loop fusion | flops 57802496 | bytes 40410112 | tf_op jit(solution)/shard_map/reduce_sum | solution.py:65
  364.3 1.7 multiply_reduce_fusion.1
  366.1 2.8 fusion.136
  368.9 146.0 %all-gather.3.cloned.1.call-done = bf16[256,6,3072]{2,1,0:T(8,128)(2,1)} async-done(((bf16[1,6,3072]{2,1,0:T(8,128)(2,1)}), bf16[256,6,3072]{2,1,0:T(8,128)(2,1)}) %all-gather.3.cloned.1.call-update) | async-done | bytes 9437200 | tf_op jit(solution)/shard_map/all_gather | solution.py:73
  514.9 14.2 %reshape.802 = bf16[1536,3072]{1,0:T(8,128)(2,1)} reshape(bf16[256,6,3072]{2,1,0:T(8,128)(2,1)} %all-gather.3.cloned.1.call-done) | data formatting | bytes 18874368
  529.1 8.5 fusion.141
  537.7 15.0 %reshape.745 = bf16[3072,1536]{1,0:T(8,128)(2,1)} reshape(bf16[256,12,1536]{2,1,0:T(8,128)(2,1)} %all-to-all-done) | data formatting | bytes 18874368 | tf_op jit(solution)/shard_map/reshape | solution.py:74
  552.7 8.5 fusion.7
  561.2 2.7 reshape.746
  563.9 1.8 reduce_sum.544
  565.9 47.5 %all_gather.7 = bf16[16,2,8,1536]{3,2,1,0:T(8,128)(2,1)S(1)} all-gather(bf16[1,2,8,1536]{3,2,1,0:T(8,128)(2,1)S(1)} %fusion.149), channel_id=1, replica_groups=mesh['dp'=16,'rows'=16] {'dp'}, dimensions={0}, use_global_device_ids=true | all-gather | bytes 835584 | tf_op jit(solution)/shard_map/all_gather | solution.py:96
  615.2 1.7 fusion.8
  617.6 87.4 %psum.15 = f32[]{:T(128)} all-reduce(f32[]{:T(128)} %subtract_reduce_fusion), channel_id=1, replica_groups=mesh['dp'=16,'rows'=16] {'dp','rows'}, use_global_device_ids=true, to_apply=%region_62.63 | all-reduce | flops 1 | bytes 8 | tf_op jit(solution)/shard_map/psum | solution.py:159
  705.6 5.8 reduce-scatter.2.cloned.1.call-done
  711.4 1.6 convolution_add_fusion
  714.3 2.3 convert_element_type.1165
  716.6 12.2 %fusion.156 = (f32[256]{0:T(256)S(1)}, f32[256]{0:T(256)S(1)}, f32[256,1536]{1,0:T(8,128)}) fusion(f32[256,1536]{1,0:T(8,128)} %fusion.136, f32[1536]{0:T(1024)S(1)} %copy-done.75, bf16[1536,3072]{1,0:T(8,128)(2,1)} %reshape.802, bf16[256,1536]{1,0:T(8,128)(2,1)} %convert_element_type.1165, bf16[3072,1536]{1,0:T(8,128)(2,1)} %reshape.745, ...), kind=kOutput, calls=%fused_computation.365 | convolution fusion | flops 4841275392 | bytes 25960448 | tf_op jit(solution)/shard_map/dot_general | solution.py:140
  728.9 6.8 fusion.135
  735.7 3.1 fusion.132
  738.8 4.6 fusion.114
  744.8 1.9 reshape_reshape.3
  747.6 4.6 collective-permute-start.3
  752.2 2.4 collective-permute-start.2
  806.5 12.1 %add_convert_fusion = bf16[1,8,32,1536]{3,2,1,0:T(8,128)(2,1)} fusion(f32[1,8,32,1536]{3,2,1,0:T(8,128)S(1)} %reshape_reshape.3, bf16[1,8,32,1536]{3,2,1,0:T(8,128)(2,1)S(1)} %bitcast.108, bf16[1,3,32,1536]{3,2,1,0:T(8,128)(2,1)S(1)} %collective-permute-done.3, bf16[1,3,32,1536]{3,2,1,0:T(8,128)(2,1)S(1)} %collective-permute-done.2, ...), kind=kLoop, calls=%fused_computation.250 | loop fusion | flops 60555264 | bytes 37066752 | tf_op jit(solution)/shard_map/convert_element_type | solution.py:155
  818.6 234.1 %all-reduce.4.cloned.1.call-done = f32[7,7,1536]{2,1,0:T(8,128)} async-done(((f32[7,7,1536]{2,1,0:T(8,128)}), f32[7,7,1536]{2,1,0:T(8,128)}) %all-reduce.4.cloned.1.call-update) | async-done | bytes 301072 | tf_op jit(solution)/shard_map/psum | solution.py:159
  1052.7 1.7 copy.48
  (261 shorter events, 61.4 us)
Async XLA Ops:
  7.2 507.7 %all-gather.3.cloned.1.call-start = ((), (), s32[]{:S(2)}) async-start(), calls=%async_computation.4 | async-start | bytes 12632064 | tf_op jit(solution)/shard_map/all_gather | solution.py:73
  14.8 522.9 %all-to-all-start = ((bf16[256,12,1536]{2,1,0:T(8,128)(2,1)}), bf16[256,12,1536]{2,1,0:T(8,128)(2,1)}, u32[]{:S(2)}, u32[]{:S(2)}) async-start(bf16[256,12,1536]{2,1,0:T(8,128)(2,1)} %stack.130), calls=%async_computation | async-start | bytes 25165824 | tf_op jit(solution)/shard_map/all_to_all | solution.py:75
  31.3 680.0 %reduce-scatter.2.cloned.1.call-start = ((), (), s32[]{:S(2)}) async-start(), calls=%async_computation.2 | async-start | bytes 835584 | tf_op jit(solution)/shard_map/reduce_scatter | solution.py:124
  31.4 318.1 %collective-permute-start.1 = (bf16[1,3,32,1536]{3,2,1,0:T(8,128)(2,1)S(1)}, bf16[1,3,32,1536]{3,2,1,0:T(8,128)(2,1)S(1)}, u32[]{:S(2)}, u32[]{:S(2)}) collective-permute-start(bf16[1,3,32,1536]{3,2,1,0:T(8,128)(2,1)S(1)} %get-tuple-element.120), channel_id=1, source_target_pairs={{1,0},{2,1},{3,2},{4,3},{5,4},{6,5},{7,6},{8,7},{9,8},{10,9},{11,1... | collective-permute-start | bytes 884744 | tf_op jit(solution)/shard_map/ppermute | solution.py:24
  35.5 307.8 %collective-permute-start = (bf16[1,3,32,1536]{3,2,1,0:T(8,128)(2,1)S(1)}, bf16[1,3,32,1536]{3,2,1,0:T(8,128)(2,1)S(1)}, u32[]{:S(2)}, u32[]{:S(2)}) collective-permute-start(bf16[1,3,32,1536]{3,2,1,0:T(8,128)(2,1)S(1)} %get-tuple-element.119), channel_id=1, source_target_pairs={{0,1},{1,2},{2,3},{3,4},{4,5},{5,6},{6,7},{7,8},{8,9},{9,10},{10,1... | collective-permute-start | bytes 884744 | tf_op jit(solution)/shard_map/ppermute | solution.py:22
  40.2 309.9 %copy-start.10 = (f32[1536]{0:T(1024)}, f32[1536]{0:T(1024)S(1)}, u32[]{:S(2)}) copy-start(f32[1536]{0:T(1024)S(1)} %get-tuple-element.70) | copy-start | bytes 18436
  40.2 309.9 %copy-start.12 = (f32[1536]{0:T(1024)}, f32[1536]{0:T(1024)S(1)}, u32[]{:S(2)}) copy-start(f32[1536]{0:T(1024)S(1)} %get-tuple-element.71) | copy-start | bytes 18436
  40.2 309.9 %copy-start.14 = (f32[1536]{0:T(1024)}, f32[1536]{0:T(1024)S(1)}, u32[]{:S(2)}) copy-start(f32[1536]{0:T(1024)S(1)} %get-tuple-element.72) | copy-start | bytes 18436
  40.2 309.9 %copy-start.16 = (f32[1536]{0:T(1024)}, f32[1536]{0:T(1024)S(1)}, u32[]{:S(2)}) copy-start(f32[1536]{0:T(1024)S(1)} %get-tuple-element.73) | copy-start | bytes 18436
  40.2 309.9 %copy-start.18 = (f32[1536]{0:T(1024)}, f32[1536]{0:T(1024)S(1)}, u32[]{:S(2)}) copy-start(f32[1536]{0:T(1024)S(1)} %get-tuple-element.74) | copy-start | bytes 18436
  40.2 309.9 %copy-start.20 = (f32[1536]{0:T(1024)}, f32[1536]{0:T(1024)S(1)}, u32[]{:S(2)}) copy-start(f32[1536]{0:T(1024)S(1)} %get-tuple-element.75) | copy-start | bytes 18436
  40.2 309.9 %copy-start.22 = (f32[1536]{0:T(1024)}, f32[1536]{0:T(1024)S(1)}, u32[]{:S(2)}) copy-start(f32[1536]{0:T(1024)S(1)} %get-tuple-element.76) | copy-start | bytes 18436
  40.2 309.9 %copy-start.24 = (f32[1536]{0:T(1024)}, f32[1536]{0:T(1024)S(1)}, u32[]{:S(2)}) copy-start(f32[1536]{0:T(1024)S(1)} %get-tuple-element.77) | copy-start | bytes 18436
  40.3 309.9 %copy-start.26 = (f32[1536]{0:T(1024)}, f32[1536]{0:T(1024)S(1)}, u32[]{:S(2)}) copy-start(f32[1536]{0:T(1024)S(1)} %get-tuple-element.78) | copy-start | bytes 18436
  40.3 309.9 %copy-start.28 = (f32[1536]{0:T(1024)}, f32[1536]{0:T(1024)S(1)}, u32[]{:S(2)}) copy-start(f32[1536]{0:T(1024)S(1)} %get-tuple-element.79) | copy-start | bytes 18436
  40.3 309.9 %copy-start.30 = (f32[1536]{0:T(1024)}, f32[1536]{0:T(1024)S(1)}, u32[]{:S(2)}) copy-start(f32[1536]{0:T(1024)S(1)} %get-tuple-element.80) | copy-start | bytes 18436
  40.3 309.9 %copy-start.32 = (f32[1536]{0:T(1024)}, f32[1536]{0:T(1024)S(1)}, u32[]{:S(2)}) copy-start(f32[1536]{0:T(1024)S(1)} %get-tuple-element.81) | copy-start | bytes 18436
  40.6 309.6 %copy-start.34 = (f32[1536]{0:T(1024)}, f32[1536]{0:T(1024)S(1)}, u32[]{:S(2)}) copy-start(f32[1536]{0:T(1024)S(1)} %get-tuple-element.82) | copy-start | bytes 18436
  40.6 309.6 %copy-start.36 = (f32[1536]{0:T(1024)}, f32[1536]{0:T(1024)S(1)}, u32[]{:S(2)}) copy-start(f32[1536]{0:T(1024)S(1)} %get-tuple-element.83) | copy-start | bytes 18436
  40.6 309.6 %copy-start.38 = (f32[1536]{0:T(1024)}, f32[1536]{0:T(1024)S(1)}, u32[]{:S(2)}) copy-start(f32[1536]{0:T(1024)S(1)} %get-tuple-element.84) | copy-start | bytes 18436
  40.6 309.6 %copy-start.40 = (f32[1536]{0:T(1024)}, f32[1536]{0:T(1024)S(1)}, u32[]{:S(2)}) copy-start(f32[1536]{0:T(1024)S(1)} %get-tuple-element.85) | copy-start | bytes 18436
  40.7 309.6 %copy-start.42 = (f32[1536]{0:T(1024)}, f32[1536]{0:T(1024)S(1)}, u32[]{:S(2)}) copy-start(f32[1536]{0:T(1024)S(1)} %get-tuple-element.86) | copy-start | bytes 18436
  40.7 309.6 %copy-start.44 = (f32[1536]{0:T(1024)}, f32[1536]{0:T(1024)S(1)}, u32[]{:S(2)}) copy-start(f32[1536]{0:T(1024)S(1)} %get-tuple-element.87) | copy-start | bytes 18436
  40.7 309.6 %copy-start.46 = (f32[1536]{0:T(1024)}, f32[1536]{0:T(1024)S(1)}, u32[]{:S(2)}) copy-start(f32[1536]{0:T(1024)S(1)} %get-tuple-element.88) | copy-start | bytes 18436
  40.7 309.6 %copy-start.48 = (f32[1536]{0:T(1024)}, f32[1536]{0:T(1024)S(1)}, u32[]{:S(2)}) copy-start(f32[1536]{0:T(1024)S(1)} %get-tuple-element.89) | copy-start | bytes 18436
  40.7 309.6 %copy-start.50 = (f32[1536]{0:T(1024)}, f32[1536]{0:T(1024)S(1)}, u32[]{:S(2)}) copy-start(f32[1536]{0:T(1024)S(1)} %get-tuple-element.90) | copy-start | bytes 18436
  40.7 309.6 %copy-start.52 = (f32[1536]{0:T(1024)}, f32[1536]{0:T(1024)S(1)}, u32[]{:S(2)}) copy-start(f32[1536]{0:T(1024)S(1)} %get-tuple-element.91) | copy-start | bytes 18436
  40.7 309.6 %copy-start.54 = (f32[1536]{0:T(1024)}, f32[1536]{0:T(1024)S(1)}, u32[]{:S(2)}) copy-start(f32[1536]{0:T(1024)S(1)} %get-tuple-element.92) | copy-start | bytes 18436
  40.7 309.6 %copy-start.56 = (f32[1536]{0:T(1024)}, f32[1536]{0:T(1024)S(1)}, u32[]{:S(2)}) copy-start(f32[1536]{0:T(1024)S(1)} %get-tuple-element.93) | copy-start | bytes 18436
  616.9 435.8 %all-reduce.4.cloned.1.call-start = ((), (), s32[]{:S(2)}) async-start(), calls=%async_computation.3 | async-start | bytes 688128 | tf_op jit(solution)/shard_map/psum | solution.py:159
  747.6 58.0 %collective-permute-start.3 = (bf16[1,3,32,1536]{3,2,1,0:T(8,128)(2,1)}, bf16[1,3,32,1536]{3,2,1,0:T(8,128)(2,1)S(1)}, u32[]{:S(2)}, u32[]{:S(2)}) collective-permute-start(bf16[1,3,32,1536]{3,2,1,0:T(8,128)(2,1)} %get-tuple-element.116), channel_id=1, source_target_pairs={{1,0},{2,1},{3,2},{4,3},{5,4},{6,5},{7,6},{8,7},{9,8},{10,9},{11,1... | collective-permute-start | bytes 884744 | tf_op jit(solution)/shard_map/ppermute | solution.py:24
  752.2 53.5 %collective-permute-start.2 = (bf16[1,3,32,1536]{3,2,1,0:T(8,128)(2,1)}, bf16[1,3,32,1536]{3,2,1,0:T(8,128)(2,1)S(1)}, u32[]{:S(2)}, u32[]{:S(2)}) collective-permute-start(bf16[1,3,32,1536]{3,2,1,0:T(8,128)(2,1)} %get-tuple-element.115), channel_id=1, source_target_pairs={{0,1},{1,2},{2,3},{3,4},{4,5},{5,6},{6,7},{7,8},{8,9},{9,10},{10,1... | collective-permute-start | bytes 884744 | tf_op jit(solution)/shard_map/ppermute | solution.py:22
  (53 other events, 2541.6 us)
Sparse Core Ops, SparseCore 0:
  9.9 505.0 all-gather.2
  617.0 94.2 reduce-scatter.1
  805.4 247.1 all-reduce.3
